TPU v7x, 128 devices: a whole 4x4x4 slice. The times are simulated.
128 devices in a mesh: region: 32 (over x, z, core), basis: 4 (over y).
Axes of the slice: x: 4, y: 4, z: 4, core: 2. Of those that a mesh axis runs over, the one named last changes fastest.
Arguments:
- observations: bfloat16 [1048576, 128], P(('region', 'basis')), may hold values from -3 to 4
- basis_values: bfloat16 [1048576, 1024], P(('region', 'basis')), as said below
- mixing: bfloat16 [1024, 1024], P('basis'), may hold values from -0.1875 to 0.1875
- pattern: int32 [8, 8], replicated, may hold values 0 or 1
- decays: float32 [32, 1024], P('region', 'basis'), may hold values from 0 to 1
- loadings: float32 [1024], P('basis'), may hold values from 0.3 to 3
Outputs:
- obs_grad: bfloat16 [1048576, 128], P(('region', 'basis'))
- attenuation_slope: float32 [32, 1024], P('region', 'basis')
Inputs may be any that keep to these rules, and one draw needn't show every extreme that they name: `basis_values`: every entry lies within 3.5 / 32768 ** 0.5 of zero.
All inputs are finite; a program needn't handle non-finite values.
Results may differ from a plain program's by a relative error of at most 0.015.
Values may be sent and summed in bfloat16 or wider, within the bound.
No kernel may reach another device: no remote copies, remote signals or barrier semaphores. Data moves between devices by JAX's collectives and lax.ppermute only.
A program may use at most 128 MiB of HBM per device.

v0:
```python
import jax
import jax.numpy as jnp
from jax import lax
from jax.sharding import PartitionSpec as P

BLOCK = 128


def entering(value, axis, join, neutral, backward):
    count, mine = (lax.axis_size(axis), lax.axis_index(axis))
    pieces = jax.tree.map(lambda part: lax.all_gather(part, axis), value)
    if backward:
        pieces = jax.tree.map(lambda part: part[::-1], pieces)
        mine = count - 1 - mine
    subtotal = jax.tree.map(
        lambda part, zero: jnp.full_like(part, 0) + jnp.asarray(zero, part.dtype), value, neutral
    )

    def turn(position, subtotal):
        longer = join(subtotal, jax.tree.map(lambda part: part[position], pieces))
        return jax.tree.map(lambda new, old: jnp.where(position < mine, new, old), longer, subtotal)

    return lax.fori_loop(0, count - 1, turn, subtotal)


def contract_rows(first_operand, second_operand):
    return lax.dot_general(
        first_operand, second_operand, (((0,), (0,)), ((), ())), preferred_element_type=jnp.float32
    )


def block_rows(mixing, pattern, owner):
    row_count = mixing.shape[0]
    width = mixing.shape[1]
    row_ids = owner * row_count + jnp.arange(row_count)
    column_index = jnp.arange(width)
    labels = jnp.arange(pattern.shape[0])
    row_hot = ((row_ids // BLOCK)[:, None] == labels[None, :]).astype(jnp.float32)
    column_hot = ((column_index // BLOCK)[:, None] == labels[None, :]).astype(jnp.float32)
    expanded = jnp.dot(jnp.dot(row_hot, pattern.astype(jnp.float32)), column_hot.T)
    identity = (row_ids[:, None] == column_index[None, :]).astype(jnp.float32)
    return (identity + mixing.astype(jnp.float32) * expanded).astype(jnp.bfloat16)


def combine(earlier, later):
    return (earlier[0] * later[0], later[0][:, None] * earlier[1] + later[1])


def shards(observations, basis_values, mixing, pattern, decays, loadings):
    owner = lax.axis_index("basis")
    share = mixing.shape[0]
    characteristics = observations.shape[1]
    mixer_rows = block_rows(mixing, pattern, owner)
    rates = decays[0]
    zero_share = jnp.zeros((share, characteristics), jnp.float32)
    identity_pair = (jnp.ones((share,), jnp.float32), zero_share)

    def predict_piece(piece):
        return jnp.dot(basis_values, piece, preferred_element_type=jnp.float32)

    summary = lax.psum_scatter(
        contract_rows(basis_values, observations), "basis", scatter_dimension=0, tiled=True
    )
    mixed_terms = jnp.dot(
        mixer_rows,
        lax.all_gather(summary.astype(jnp.bfloat16), "basis", axis=0, tiled=True),
        preferred_element_type=jnp.float32,
    )
    _, previous = entering((rates, mixed_terms), "region", combine, identity_pair, False)
    states = rates[:, None] * previous + mixed_terms
    loaded_values = (loadings[:, None] * states).astype(jnp.bfloat16)
    fitted = predict_piece(lax.all_gather(loaded_values, "basis", axis=0, tiled=True))
    residual = (fitted - observations.astype(jnp.float32)).astype(jnp.bfloat16)
    pulled = loadings[:, None] * lax.psum_scatter(
        contract_rows(basis_values, residual).astype(jnp.bfloat16),
        "basis",
        scatter_dimension=0,
        tiled=True,
    ).astype(jnp.float32)
    _, carried = entering((rates, rates[:, None] * pulled), "region", combine, identity_pair, True)
    adjoints = pulled + carried
    attenuation_slope = (jnp.sum(adjoints * previous, axis=1) / characteristics)[None, :]
    adjoint_b = adjoints.astype(jnp.bfloat16)
    back_owned = lax.psum_scatter(
        contract_rows(mixer_rows, adjoint_b), "basis", scatter_dimension=0, tiled=True
    ).astype(jnp.bfloat16)
    spread = predict_piece(lax.all_gather(back_owned, "basis", axis=0, tiled=True))
    obs_grad = (spread - residual.astype(jnp.float32)).astype(jnp.bfloat16)
    return (obs_grad, attenuation_slope)


def solution(mesh):
    in_specs = (
        P(("region", "basis"), None),
        P(("region", "basis"), None),
        P("basis", None),
        P(),
        P("region", "basis"),
        P("basis"),
    )
    out_specs = (P(("region", "basis"), None), P("region", "basis"))
    return jax.shard_map(shards, mesh=mesh, in_specs=in_specs, out_specs=out_specs, check_vma=False)
```

profile of v0, /device:TPU:0, one launch (start us, length us, event | category | flops | bytes accessed | tf_op | source)
XLA Modules:
  0.0 337.9 jit_solution(7736925620875022976)
XLA Ops:
  7.2 11.7 %fusion.25 = f32[1024,128]{1,0:T(8,128)} fusion(bf16[8192,1024]{1,0:T(8,128)(2,1)} %param.11, bf16[8192,128]{1,0:T(8,128)(2,1)} %param.10), kind=kOutput, calls=%fused_computation.46 | convolution fusion | flops 2147483648 | bytes 19398656 | tf_op jit(solution)/shard_map/dot_general | solution.py:27
  19.0 1.7 fusion.7
  20.7 22.3 %reduce-scatter.4.cloned.1.call-done = f32[256,128]{1,0:T(8,128)} async-done(((f32[1024,128]{1,0:T(8,128)}), f32[256,128]{1,0:T(8,128)}) %reduce-scatter.4.cloned.1.call-update) | async-done | bytes 131088 | tf_op jit(solution)/shard_map/reduce_scatter | solution.py:61
  43.9 12.2 %all_gather.26 = bf16[1024,128]{1,0:T(8,128)(2,1)S(1)} all-gather(bf16[256,128]{1,0:T(8,128)(2,1)S(1)} %convert_element_type.51), channel_id=1, replica_groups=mesh['region'=32,'basis'=4] {'basis'}, dimensions={0}, use_global_device_ids=true | all-gather | bytes 327680 | tf_op jit(solution)/shard_map/all_gather | solution.py:66
  57.2 2.9 copy.11
  60.1 24.3 %all-gather.2 = f32[32,1,256]{2,1,0:T(1,128)S(1)} all-gather(f32[1,1,256]{2,1,0:T(1,128)S(1)} %bitcast.56), channel_id=1, replica_groups=mesh['region'=32,'basis'=4] {'region'}, dimensions={0}, use_global_device_ids=true | all-gather | bytes 33792 | tf_op jit(solution)/shard_map/all_gather | solution.py:11
  84.4 19.0 %all-gather.6.cloned.1.call-done = f32[8192,128]{1,0:T(8,128)} async-done(((f32[256,128]{1,0:T(8,128)}), f32[8192,128]{1,0:T(8,128)}) %all-gather.6.cloned.1.call-update) | async-done | bytes 4194320 | tf_op jit(solution)/shard_map/all_gather | solution.py:11
  103.4 33.2 %while.28 = (s32[]{:T(128)}, f32[256,128]{1,0:T(8,128)S(1)}, s32[]{:T(128)}, f32[32,256]{1,0:T(8,128)S(1)}, f32[32,256,128]{2,1,0:T(8,128)}, /*index=5*/s32[]{:T(128)}, s32[]{:T(128)}) while((s32[]{:T(128)}, f32[256,128]{1,0:T(8,128)S(1)}, s32[]{:T(128)}, f32[32,256]{1,0:T(8,128)S(1)}, f32[32,256,128]{2,1,0:T(8,128)}, ...), condition=%wide.region_2.3_spmd.clone, body=%wide.region_1.2_spmd.clone.sunk | while | flops 131076 | bytes 396393 | solution.py:23
  104.4 1.0 fusion.40
  105.5 1.0 fusion.40
  106.6 1.0 fusion.40
  107.7 1.0 fusion.40
  108.7 1.0 fusion.40
  109.8 1.0 fusion.40
  110.9 1.0 fusion.40
  111.9 1.0 fusion.40
  114.1 1.0 fusion.40
  134.4 1.0 fusion.40
  136.7 12.8 %all_gather.29 = bf16[1024,128]{1,0:T(8,128)(2,1)S(1)} all-gather(bf16[256,128]{1,0:T(8,128)(2,1)S(1)} %multiply_convert_fusion), channel_id=1, replica_groups=mesh['region'=32,'basis'=4] {'basis'}, dimensions={0}, use_global_device_ids=true | all-gather | bytes 327680 | tf_op jit(solution)/shard_map/all_gather | solution.py:72
  149.5 12.0 %fusion.5 = bf16[8192,128]{0,1:T(8,128)(2,1)S(1)} fusion(bf16[1024,128]{1,0:T(8,128)(2,1)S(1)} %all_gather.29, bf16[8192,1024]{1,0:T(8,128)(2,1)} %param.11, bf16[8192,128]{0,1:T(8,128)(2,1)} %copy.11), kind=kOutput, calls=%fused_computation.11 | convolution fusion | flops 2150629376 | bytes 21233664 | tf_op jit(solution)/shard_map/dot_general | solution.py:59
  161.5 10.8 %fusion.8 = bf16[1024,128]{1,0:T(8,128)(2,1)} fusion(bf16[8192,128]{0,1:T(8,128)(2,1)S(1)} %fusion.5, bf16[8192,1024]{1,0:T(8,128)(2,1)} %param.11), kind=kOutput, calls=%fused_computation.16 | convolution fusion | flops 2147614720 | bytes 19136512 | tf_op jit(solution)/shard_map/dot_general | solution.py:27
  172.4 19.7 %reduce-scatter.6.cloned.1.call-done = bf16[256,128]{1,0:T(8,128)(2,1)} async-done(((bf16[1024,128]{1,0:T(8,128)(2,1)}), bf16[256,128]{1,0:T(8,128)(2,1)}) %reduce-scatter.6.cloned.1.call-update) | async-done | bytes 65552 | tf_op jit(solution)/shard_map/reduce_scatter | solution.py:74
  192.1 1.6 fusion.13
  193.9 47.3 %all-gather.8.cloned.1.call-done = f32[8192,128]{1,0:T(8,128)} async-done(((f32[256,128]{1,0:T(8,128)}), f32[8192,128]{1,0:T(8,128)}) %all-gather.8.cloned.1.call-update) | async-done | bytes 4194320 | tf_op jit(solution)/shard_map/all_gather | solution.py:11
  241.2 4.6 %rev.7 = f32[32,256,128]{2,1,0:T(8,128)} reverse(f32[32,256,128]{2,1,0:T(8,128)} %bitcast.51), dimensions={0} | reverse | bytes 8388608 | tf_op jit(solution)/shard_map/rev | solution.py:13
  245.9 33.2 %while.29 = (s32[]{:T(128)}, f32[256,128]{1,0:T(8,128)S(1)}, s32[]{:T(128)}, f32[32,256]{1,0:T(8,128)S(1)}, f32[32,256,128]{2,1,0:T(8,128)}, /*index=5*/s32[]{:T(128)}, s32[]{:T(128)}) while((s32[]{:T(128)}, f32[256,128]{1,0:T(8,128)S(1)}, s32[]{:T(128)}, f32[32,256]{1,0:T(8,128)S(1)}, f32[32,256,128]{2,1,0:T(8,128)}, ...), condition=%wide.region_5.6_spmd.clone, body=%wide.region_4.5_spmd.clone.sunk | while | flops 131076 | bytes 396393 | solution.py:23
  260.9 1.0 fusion.41
  279.1 1.2 fusion.15
  281.0 20.1 %reduce-scatter.8.cloned.1.call-done = f32[256,128]{1,0:T(8,128)} async-done(((f32[1024,128]{1,0:T(8,128)}), f32[256,128]{1,0:T(8,128)}) %reduce-scatter.8.cloned.1.call-update) | async-done | bytes 131088 | tf_op jit(solution)/shard_map/reduce_scatter | solution.py:84
  302.1 12.5 %all_gather.32 = bf16[1024,128]{1,0:T(8,128)(2,1)S(1)} all-gather(bf16[256,128]{1,0:T(8,128)(2,1)S(1)} %convert_element_type.59), channel_id=1, replica_groups=mesh['region'=32,'basis'=4] {'basis'}, dimensions={0}, use_global_device_ids=true | all-gather | bytes 327680 | tf_op jit(solution)/shard_map/all_gather | solution.py:87
  314.5 12.8 %fusion.4 = bf16[8192,128]{0,1:T(8,128)(2,1)} fusion(bf16[1024,128]{1,0:T(8,128)(2,1)S(1)} %all_gather.32, bf16[8192,1024]{1,0:T(8,128)(2,1)} %param.11, bf16[8192,128]{0,1:T(8,128)(2,1)S(1)} %fusion.5), kind=kOutput, calls=%fused_computation.10 | convolution fusion | flops 2150629376 | bytes 21233664 | tf_op jit(solution)/shard_map/dot_general | solution.py:59
  327.3 4.1 %copy.13 = bf16[8192,128]{1,0:T(8,128)(2,1)} copy(bf16[8192,128]{0,1:T(8,128)(2,1)} %fusion.4) | data formatting | bytes 4194304
  (147 shorter events, 57.1 us)
Async XLA Ops:
  7.2 11.8 %copy-start.5 = (s32[8,8]{1,0:T(8,128)S(1)}, s32[8,8]{1,0:T(8,128)}, u32[]{:S(2)}) copy-start(s32[8,8]{1,0:T(8,128)} %param.13) | copy-start | bytes 772
  7.2 35.8 %reduce-scatter.4.cloned.1.call-start = ((), (), s32[]{:S(2)}) async-start(), calls=%async_computation.3 | async-start | bytes 655360 | tf_op jit(solution)/shard_map/reduce_scatter | solution.py:61
  18.9 38.3 %copy-start = (bf16[8192,128]{1,0:T(8,128)(2,1)S(1)}, bf16[8192,128]{1,0:T(8,128)(2,1)}, u32[]{:S(2)}) copy-start(bf16[8192,128]{1,0:T(8,128)(2,1)} %param.10) | copy-start | bytes 6291460
  18.9 41.2 %copy-start.4 = (f32[1,256]{1,0:T(1,128)S(1)}, f32[1,256]{1,0:T(1,128)}, u32[]{:S(2)}) copy-start(f32[1,256]{1,0:T(1,128)} %param.14) | copy-start | bytes 3076
  18.9 84.4 %all-gather.6.cloned.1.call-start = ((), (), s32[]{:S(2)}) async-start(), calls=%async_computation.6 | async-start | bytes 4325376 | tf_op jit(solution)/shard_map/all_gather | solution.py:11
  20.7 115.9 %copy-start.3 = (f32[256]{0:T(256)S(1)}, f32[256]{0:T(256)}, u32[]{:S(2)}) copy-start(f32[256]{0:T(256)} %param.15) | copy-start | bytes 3076
  57.1 79.5 %copy-start.1 = (f32[256,128]{1,0:T(8,128)S(1)}, f32[256,128]{1,0:T(8,128)}, u32[]{:S(2)}) copy-start(f32[256,128]{1,0:T(8,128)} %fusion.26) | copy-start | bytes 393220
  57.1 135.1 %reduce-scatter.6.cloned.1.call-start = ((), (), s32[]{:S(2)}) async-start(), calls=%async_computation.4 | async-start | bytes 327680 | tf_op jit(solution)/shard_map/reduce_scatter | solution.py:74
  172.4 68.8 %all-gather.8.cloned.1.call-start = ((), (), s32[]{:S(2)}) async-start(), calls=%async_computation.7 | async-start | bytes 4325376 | tf_op jit(solution)/shard_map/all_gather | solution.py:11
  193.8 107.4 %reduce-scatter.8.cloned.1.call-start = ((), (), s32[]{:S(2)}) async-start(), calls=%async_computation.5 | async-start | bytes 655360 | tf_op jit(solution)/shard_map/reduce_scatter | solution.py:84
  241.2 37.8 %copy-start.2 = (bf16[256,128]{1,0:T(8,128)(2,1)S(1)}, bf16[256,128]{1,0:T(8,128)(2,1)}, u32[]{:S(2)}) copy-start(bf16[256,128]{1,0:T(8,128)(2,1)} %reduce-scatter.6.cloned.1.call-done) | copy-start | bytes 196612
Sparse Core Ops, SparseCore 0:
  19.0 23.8 reduce-scatter.3
  57.2 46.1 all-gather.5
  172.5 19.6 reduce-scatter.5
  195.1 46.0 all-gather.7
  280.4 20.7 reduce-scatter.7
where the time goes:
time: 339 us; the launch traced here: 338 us
  waiting for transfers between devices  128 us (38%)
  other arithmetic  68.1 us (20%)
  blocking collectives  61.8 us (18%)
  matrix products  51.1 us (15%)
  between operations  13.9 us (4%)
  local copies, waits for them, and re-layouts  12.3 us (4%)
    all_gather x2, waiting for transfers between devices, entering(): pieces = jax.tree.map(lambda part: lax.all_gather(part, axis), value)  66.3 us
    select_n x62, other arithmetic, turn(): jnp.where(position < mine, new, old)  63.8 us
    dot_general x2, matrix products, predict_piece(): return jnp.dot(basis_values, piece, preferred_element_type=jnp.float32)  24.8 us
    all_gather x1, blocking collectives, entering(): pieces = jax.tree.map(lambda part: lax.all_gather(part, axis), value)  24.3 us
    dot_general x3, matrix products, contract_rows(): lax.dot_general(first_operand, second_operand, (((0,), (0,)), ((), ())),...  23.7 us
    reduce_scatter x1, waiting for transfers between devices, shards(): lax.psum_scatter(contract_rows(basis_values, observations), 'basis', scat...  22.3 us
    reduce_scatter x1, waiting for transfers between devices, shards(): lax.psum_scatter(contract_rows(mixer_rows, adjoint_b), 'basis', scatter_d...  20.1 us
    reduce_scatter x1, waiting for transfers between devices, shards(): lax.psum_scatter(contract_rows(basis_values, residual).astype(jnp.bfloat1...  19.7 us
  transfers between devices with their start and end apart: 5, of which 5 were waited for; matrix products, arithmetic and copies ran while one was open for 2% of the time, Pallas kernels for 0%

commit v1 on v0

--- a/solution.py
+++ b/solution.py
@@ -4,6 +4,16 @@
 from jax.sharding import PartitionSpec as P
 
 BLOCK = 128
+
+
+def _guide_shapes(block_in):
+    local_now = jnp.concatenate(
+        lax.all_to_all(
+            jnp.stack([block_in for _ in range(lax.axis_size("basis"))], 0), "basis", 0, 0
+        ),
+        0,
+    )
+    return local_now
 
 
 def entering(value, axis, join, neutral, backward):
@@ -62,9 +72,7 @@
         contract_rows(basis_values, observations), "basis", scatter_dimension=0, tiled=True
     )
     mixed_terms = jnp.dot(
-        mixer_rows,
-        lax.all_gather(summary.astype(jnp.bfloat16), "basis", axis=0, tiled=True),
-        preferred_element_type=jnp.float32,
+        mixer_rows, _guide_shapes(summary.astype(jnp.bfloat16)), preferred_element_type=jnp.float32
     )
     _, previous = entering((rates, mixed_terms), "region", combine, identity_pair, False)
     states = rates[:, None] * previous + mixed_terms

time: 339 us -> 338 us (level)
  blocking collectives: 61.8 us -> 49.6 us
  waiting for transfers between devices: 128 us -> 135 us
  starting transfers between devices: 0.21 us -> 3.61 us
    all_gather x1 -> x0, blocking collectives: 12.2 us -> none  [shards(): lax.all_gather(summary.astype(jnp.bfloat16), 'basis', axis=0, tiled=True)]
    all_to_all x0 -> x1, waiting for transfers between devices: none -> 5.02 us  [_guide_shapes(): lax.all_to_all(jnp.stack([block_in for _ in range(lax.axis_size('basis'))...]
    all_to_all x0 -> x1, starting transfers between devices: none -> 3.41 us  [_guide_shapes(): lax.all_to_all(jnp.stack([block_in for _ in range(lax.axis_size('basis'))...]
  transfers between devices with their start and end apart: 5 -> 6, of which waited for: 5 -> 6; matrix products, arithmetic and copies ran while one was open for 2% -> 2% of each run, Pallas kernels for 0% -> 0%
where the time goes in v1:
time: 338 us; the launch traced here: 336 us
  waiting for transfers between devices  135 us (40%)
  other arithmetic  68.1 us (20%)
  matrix products  51 us (15%)
  blocking collectives  49.6 us (15%)
  between operations  13.9 us (4%)
  local copies, waits for them, and re-layouts  13 us (4%)
  starting transfers between devices  3.61 us (1%)
    all_gather x2, waiting for transfers between devices, entering(): pieces = jax.tree.map(lambda part: lax.all_gather(part, axis), value)  66 us
    select_n x62, other arithmetic, turn(): jnp.where(position < mine, new, old)  63.8 us
    dot_general x2, matrix products, predict_piece(): return jnp.dot(basis_values, piece, preferred_element_type=jnp.float32)  24.8 us
    all_gather x1, blocking collectives, entering(): pieces = jax.tree.map(lambda part: lax.all_gather(part, axis), value)  24.3 us
    reduce_scatter x1, waiting for transfers between devices, shards(): lax.psum_scatter(contract_rows(basis_values, observations), 'basis', scat...  24 us
    dot_general x3, matrix products, contract_rows(): lax.dot_general(first_operand, second_operand, (((0,), (0,)), ((), ())),...  23.7 us
    reduce_scatter x1, waiting for transfers between devices, shards(): lax.psum_scatter(contract_rows(mixer_rows, adjoint_b), 'basis', scatter_d...  20.1 us
    reduce_scatter x1, waiting for transfers between devices, shards(): lax.psum_scatter(contract_rows(basis_values, residual).astype(jnp.bfloat1...  19.7 us
  transfers between devices with their start and end apart: 6, of which 6 were waited for; matrix products, arithmetic and copies ran while one was open for 2% of the time, Pallas kernels for 0%

profile of v1, /device:TPU:0, one launch (start us, length us, event | category | flops | bytes accessed | tf_op | source)
XLA Modules:
  0.0 336.2 jit_solution(9158178683526068367)
XLA Ops:
  7.2 11.7 %fusion.25 = f32[1024,128]{1,0:T(8,128)} fusion(bf16[8192,1024]{1,0:T(8,128)(2,1)} %param.11, bf16[8192,128]{1,0:T(8,128)(2,1)} %param.10), kind=kOutput, calls=%fused_computation.46 | convolution fusion | flops 2147483648 | bytes 19398656 | tf_op jit(solution)/shard_map/dot_general | solution.py:37
  19.0 24.0 %reduce-scatter.4.cloned.1.call-done = f32[256,128]{1,0:T(8,128)} async-done(((f32[1024,128]{1,0:T(8,128)}), f32[256,128]{1,0:T(8,128)}) %reduce-scatter.4.cloned.1.call-update) | async-done | bytes 131088 | tf_op jit(solution)/shard_map/reduce_scatter | solution.py:71
  44.6 3.4 %all-to-all-start = ((bf16[4,256,128]{2,1,0:T(8,128)(2,1)}), bf16[4,256,128]{2,1,0:T(8,128)(2,1)S(1)}, u32[]{:S(2)}, u32[]{:S(2)}) async-start(bf16[4,256,128]{2,1,0:T(8,128)(2,1)} %stack.2), calls=%async_computation.1 | async-start | bytes 524288 | tf_op jit(solution)/shard_map/all_to_all | solution.py:11
  48.1 1.5 fusion.7
  49.7 5.0 %all-to-all-done = bf16[4,256,128]{2,1,0:T(8,128)(2,1)S(1)} async-done(((bf16[4,256,128]{2,1,0:T(8,128)(2,1)}), bf16[4,256,128]{2,1,0:T(8,128)(2,1)S(1)}, u32[]{:S(2)}, u32[]{:S(2)}) %all-to-all-start) | async-done | bytes 262176 | tf_op jit(solution)/shard_map/all_to_all | solution.py:11
  55.7 2.9 copy.11
  58.6 24.3 %all-gather.2 = f32[32,1,256]{2,1,0:T(1,128)S(1)} all-gather(f32[1,1,256]{2,1,0:T(1,128)S(1)} %bitcast.58), channel_id=1, replica_groups=mesh['region'=32,'basis'=4] {'region'}, dimensions={0}, use_global_device_ids=true | all-gather | bytes 33792 | tf_op jit(solution)/shard_map/all_gather | solution.py:21
  82.9 18.7 %all-gather.6.cloned.1.call-done = f32[8192,128]{1,0:T(8,128)} async-done(((f32[256,128]{1,0:T(8,128)}), f32[8192,128]{1,0:T(8,128)}) %all-gather.6.cloned.1.call-update) | async-done | bytes 4194320 | tf_op jit(solution)/shard_map/all_gather | solution.py:21
  101.6 33.2 %while.28 = (s32[]{:T(128)}, f32[256,128]{1,0:T(8,128)S(1)}, s32[]{:T(128)}, f32[32,256]{1,0:T(8,128)S(1)}, f32[32,256,128]{2,1,0:T(8,128)}, /*index=5*/s32[]{:T(128)}, s32[]{:T(128)}) while((s32[]{:T(128)}, f32[256,128]{1,0:T(8,128)S(1)}, s32[]{:T(128)}, f32[32,256]{1,0:T(8,128)S(1)}, f32[32,256,128]{2,1,0:T(8,128)}, ...), condition=%wide.region_2.3_spmd.clone, body=%wide.region_1.2_spmd.clone.sunk | while | flops 131076 | bytes 396393 | solution.py:33
  102.7 1.0 fusion.40
  103.8 1.0 fusion.40
  104.8 1.0 fusion.40
  105.9 1.0 fusion.40
  107.0 1.0 fusion.40
  108.1 1.0 fusion.40
  109.1 1.0 fusion.40
  118.8 1.0 fusion.40
  135.0 12.8 %all_gather.25 = bf16[1024,128]{1,0:T(8,128)(2,1)S(1)} all-gather(bf16[256,128]{1,0:T(8,128)(2,1)S(1)} %multiply_convert_fusion), channel_id=1, replica_groups=mesh['region'=32,'basis'=4] {'basis'}, dimensions={0}, use_global_device_ids=true | all-gather | bytes 327680 | tf_op jit(solution)/shard_map/all_gather | solution.py:80
  147.7 12.0 %fusion.5 = bf16[8192,128]{0,1:T(8,128)(2,1)S(1)} fusion(bf16[1024,128]{1,0:T(8,128)(2,1)S(1)} %all_gather.25, bf16[8192,1024]{1,0:T(8,128)(2,1)} %param.11, bf16[8192,128]{0,1:T(8,128)(2,1)} %copy.11), kind=kOutput, calls=%fused_computation.11 | convolution fusion | flops 2150629376 | bytes 21233664 | tf_op jit(solution)/shard_map/dot_general | solution.py:69
  159.8 10.8 %fusion.8 = bf16[1024,128]{1,0:T(8,128)(2,1)} fusion(bf16[8192,128]{0,1:T(8,128)(2,1)S(1)} %fusion.5, bf16[8192,1024]{1,0:T(8,128)(2,1)} %param.11), kind=kOutput, calls=%fused_computation.16 | convolution fusion | flops 2147614720 | bytes 19136512 | tf_op jit(solution)/shard_map/dot_general | solution.py:37
  170.7 19.7 %reduce-scatter.6.cloned.1.call-done = bf16[256,128]{1,0:T(8,128)(2,1)} async-done(((bf16[1024,128]{1,0:T(8,128)(2,1)}), bf16[256,128]{1,0:T(8,128)(2,1)}) %reduce-scatter.6.cloned.1.call-update) | async-done | bytes 65552 | tf_op jit(solution)/shard_map/reduce_scatter | solution.py:82
  190.4 1.6 fusion.13
  192.2 47.3 %all-gather.8.cloned.1.call-done = f32[8192,128]{1,0:T(8,128)} async-done(((f32[256,128]{1,0:T(8,128)}), f32[8192,128]{1,0:T(8,128)}) %all-gather.8.cloned.1.call-update) | async-done | bytes 4194320 | tf_op jit(solution)/shard_map/all_gather | solution.py:21
  239.5 4.6 %rev.7 = f32[32,256,128]{2,1,0:T(8,128)} reverse(f32[32,256,128]{2,1,0:T(8,128)} %bitcast.52), dimensions={0} | reverse | bytes 8388608 | tf_op jit(solution)/shard_map/rev | solution.py:23
  244.1 33.2 %while.29 = (s32[]{:T(128)}, f32[256,128]{1,0:T(8,128)S(1)}, s32[]{:T(128)}, f32[32,256]{1,0:T(8,128)S(1)}, f32[32,256,128]{2,1,0:T(8,128)}, /*index=5*/s32[]{:T(128)}, s32[]{:T(128)}) while((s32[]{:T(128)}, f32[256,128]{1,0:T(8,128)S(1)}, s32[]{:T(128)}, f32[32,256]{1,0:T(8,128)S(1)}, f32[32,256,128]{2,1,0:T(8,128)}, ...), condition=%wide.region_5.6_spmd.clone, body=%wide.region_4.5_spmd.clone.sunk | while | flops 131076 | bytes 396393 | solution.py:33
  250.5 1.0 fusion.41
  270.9 1.0 fusion.41
  277.3 1.2 fusion.15
  279.3 20.1 %reduce-scatter.8.cloned.1.call-done = f32[256,128]{1,0:T(8,128)} async-done(((f32[1024,128]{1,0:T(8,128)}), f32[256,128]{1,0:T(8,128)}) %reduce-scatter.8.cloned.1.call-update) | async-done | bytes 131088 | tf_op jit(solution)/shard_map/reduce_scatter | solution.py:92
  300.3 12.5 %all_gather.28 = bf16[1024,128]{1,0:T(8,128)(2,1)S(1)} all-gather(bf16[256,128]{1,0:T(8,128)(2,1)S(1)} %convert_element_type.59), channel_id=1, replica_groups=mesh['region'=32,'basis'=4] {'basis'}, dimensions={0}, use_global_device_ids=true | all-gather | bytes 327680 | tf_op jit(solution)/shard_map/all_gather | solution.py:95
  312.8 12.8 %fusion.4 = bf16[8192,128]{0,1:T(8,128)(2,1)} fusion(bf16[1024,128]{1,0:T(8,128)(2,1)S(1)} %all_gather.28, bf16[8192,1024]{1,0:T(8,128)(2,1)} %param.11, bf16[8192,128]{0,1:T(8,128)(2,1)S(1)} %fusion.5), kind=kOutput, calls=%fused_computation.10 | convolution fusion | flops 2150629376 | bytes 21233664 | tf_op jit(solution)/shard_map/dot_general | solution.py:69
  325.6 4.1 %copy.13 = bf16[8192,128]{1,0:T(8,128)(2,1)} copy(bf16[8192,128]{0,1:T(8,128)(2,1)} %fusion.4) | data formatting | bytes 4194304
  (149 shorter events, 58.8 us)
Async XLA Ops:
  7.2 40.9 %copy-start.5 = (s32[8,8]{1,0:T(8,128)S(1)}, s32[8,8]{1,0:T(8,128)}, u32[]{:S(2)}) copy-start(s32[8,8]{1,0:T(8,128)} %param.13) | copy-start | bytes 772
  7.2 35.8 %reduce-scatter.4.cloned.1.call-start = ((), (), s32[]{:S(2)}) async-start(), calls=%async_computation.4 | async-start | bytes 655360 | tf_op jit(solution)/shard_map/reduce_scatter | solution.py:71
  18.9 36.8 %copy-start = (bf16[8192,128]{1,0:T(8,128)(2,1)S(1)}, bf16[8192,128]{1,0:T(8,128)(2,1)}, u32[]{:S(2)}) copy-start(bf16[8192,128]{1,0:T(8,128)(2,1)} %param.10) | copy-start | bytes 6291460
  18.9 39.7 %copy-start.4 = (f32[1,256]{1,0:T(1,128)S(1)}, f32[1,256]{1,0:T(1,128)}, u32[]{:S(2)}) copy-start(f32[1,256]{1,0:T(1,128)} %param.14) | copy-start | bytes 3076
  44.6 10.1 %all-to-all-start = ((bf16[4,256,128]{2,1,0:T(8,128)(2,1)}), bf16[4,256,128]{2,1,0:T(8,128)(2,1)S(1)}, u32[]{:S(2)}, u32[]{:S(2)}) async-start(bf16[4,256,128]{2,1,0:T(8,128)(2,1)} %stack.2), calls=%async_computation.1 | async-start | bytes 524288 | tf_op jit(solution)/shard_map/all_to_all | solution.py:11
  48.0 53.6 %all-gather.6.cloned.1.call-start = ((), (), s32[]{:S(2)}) async-start(), calls=%async_computation.7 | async-start | bytes 4325376 | tf_op jit(solution)/shard_map/all_gather | solution.py:21
  48.1 86.7 %copy-start.3 = (f32[256]{0:T(256)S(1)}, f32[256]{0:T(256)}, u32[]{:S(2)}) copy-start(f32[256]{0:T(256)} %param.15) | copy-start | bytes 3076
  55.6 79.2 %copy-start.1 = (f32[256,128]{1,0:T(8,128)S(1)}, f32[256,128]{1,0:T(8,128)}, u32[]{:S(2)}) copy-start(f32[256,128]{1,0:T(8,128)} %fusion.26) | copy-start | bytes 393220
  55.6 134.8 %reduce-scatter.6.cloned.1.call-start = ((), (), s32[]{:S(2)}) async-start(), calls=%async_computation.5 | async-start | bytes 327680 | tf_op jit(solution)/shard_map/reduce_scatter | solution.py:82
  170.6 68.8 %all-gather.8.cloned.1.call-start = ((), (), s32[]{:S(2)}) async-start(), calls=%async_computation.8 | async-start | bytes 4325376 | tf_op jit(solution)/shard_map/all_gather | solution.py:21
  192.1 107.4 %reduce-scatter.8.cloned.1.call-start = ((), (), s32[]{:S(2)}) async-start(), calls=%async_computation.6 | async-start | bytes 655360 | tf_op jit(solution)/shard_map/reduce_scatter | solution.py:92
  239.5 37.9 %copy-start.2 = (bf16[256,128]{1,0:T(8,128)(2,1)S(1)}, bf16[256,128]{1,0:T(8,128)(2,1)}, u32[]{:S(2)}) copy-start(bf16[256,128]{1,0:T(8,128)(2,1)} %reduce-scatter.6.cloned.1.call-done) | copy-start | bytes 196612
Sparse Core Ops, SparseCore 0:
  19.0 23.8 reduce-scatter.3
  55.8 45.8 all-gather.5
  170.7 19.6 reduce-scatter.5
  193.3 46.0 all-gather.7
  278.7 20.7 reduce-scatter.7
